TPU v7x, 32 devices: a whole 2x2x4 slice. The times are simulated.
32 devices in a mesh: rows: 8 (over y, x, core), tp: 4 (over z).
Axes of the slice: x: 2, y: 2, z: 4, core: 2. Of those that a mesh axis runs over, the one named last changes fastest.
Arguments:
- first_query: float32 [9216, 9216], P('rows', 'tp'), may hold values from -0.09375 to 0.09375
- second_query: float32 [9216, 9216], P('rows', 'tp'), may hold values from -0.0625 to 0.0625
- first_key: float32 [9216, 9216], P('rows', 'tp'), may hold values from -0.09375 to 0.09375
- second_key: float32 [9216, 9216], P('rows', 'tp'), may hold values from -0.0625 to 0.0625
- first_value: float32 [9216, 9216], P('rows', 'tp'), may hold values from -0.09375 to 0.09375
- second_value: float32 [9216, 9216], P('rows', 'tp'), may hold values from -0.0625 to 0.0625
- mix_share: float32 [9216], P('rows'), may hold values from 0.2 to 0.8
- norm_train: float32 [9216], P(('rows', 'tp')), may hold values from 0.25 to 1.75
- norm_step: float32 [9216], P(('rows', 'tp')), may hold values from -0.3 to 0.3
Outputs:
- serving_query: bfloat16 [9216, 9216], P(None, ('tp', 'rows'))
- serving_key: bfloat16 [9216, 9216], P(None, ('tp', 'rows'))
- serving_value: bfloat16 [9216, 9216], P(None, ('tp', 'rows'))
- scale_query: float32 [9216], P(('tp', 'rows'))
- scale_key: float32 [9216], P(('tp', 'rows'))
- scale_value: float32 [9216], P(('tp', 'rows'))
- serve_norm: bfloat16 [9216], replicated
All inputs are finite; a program needn't handle non-finite values.
Results may differ from a plain program's by a relative error of at most 0.001.
Values may be sent and summed in bfloat16 or wider, within the bound.
A program may use at most 192 MiB of HBM per device.

v0:
```python
import jax
import jax.numpy as jnp
from jax import lax
from jax.sharding import PartitionSpec as P


def per_device(
    first_query,
    second_query,
    first_key,
    second_key,
    first_value,
    second_value,
    mix_share,
    norm_train,
    norm_step,
):
    whole_query = mix_share[:, None] * first_query + (1.0 - mix_share[:, None]) * second_query
    whole_key = mix_share[:, None] * first_key + (1.0 - mix_share[:, None]) * second_key
    whole_value = mix_share[:, None] * first_value + (1.0 - mix_share[:, None]) * second_value
    scale_query, scale_key, scale_value = lax.pmax(
        (
            jnp.max(jnp.abs(whole_query), axis=0),
            jnp.max(jnp.abs(whole_key), axis=0),
            jnp.max(jnp.abs(whole_value), axis=0),
        ),
        "rows",
    )
    narrow_query, narrow_key, narrow_value = (
        (whole_query / scale_query).astype(jnp.bfloat16),
        (whole_key / scale_key).astype(jnp.bfloat16),
        (whole_value / scale_value).astype(jnp.bfloat16),
    )
    serving_query, serving_key, serving_value = (
        lax.all_to_all(narrow_query, "rows", split_axis=1, concat_axis=0, tiled=True),
        lax.all_to_all(narrow_key, "rows", split_axis=1, concat_axis=0, tiled=True),
        lax.all_to_all(narrow_value, "rows", split_axis=1, concat_axis=0, tiled=True),
    )
    place = lax.axis_index("rows")
    scale_query = lax.dynamic_slice_in_dim(
        scale_query, place * serving_query.shape[1], serving_query.shape[1]
    )
    scale_key = lax.dynamic_slice_in_dim(
        scale_key, place * serving_key.shape[1], serving_key.shape[1]
    )
    scale_value = lax.dynamic_slice_in_dim(
        scale_value, place * serving_value.shape[1], serving_value.shape[1]
    )
    serve_norm = lax.all_gather(
        (norm_train + norm_step).astype(jnp.bfloat16), ("rows", "tp"), axis=0, tiled=True
    )
    return (
        serving_query,
        serving_key,
        serving_value,
        scale_query,
        scale_key,
        scale_value,
        serve_norm,
    )


def solution(mesh):
    return jax.shard_map(
        per_device,
        mesh=mesh,
        in_specs=(
            P("rows", "tp"),
            P("rows", "tp"),
            P("rows", "tp"),
            P("rows", "tp"),
            P("rows", "tp"),
            P("rows", "tp"),
            P("rows"),
            P(("rows", "tp")),
            P(("rows", "tp")),
        ),
        out_specs=(
            P(None, ("tp", "rows")),
            P(None, ("tp", "rows")),
            P(None, ("tp", "rows")),
            P(("tp", "rows")),
            P(("tp", "rows")),
            P(("tp", "rows")),
            P(),
        ),
        check_vma=False,
    )
```

profile of v0, /device:TPU:0, one launch (start us, length us, event | category | flops | bytes accessed | tf_op | source)
XLA Modules:
  0.0 396.1 jit_solution(8847732719092262777)
XLA Ops:
  0.6 12.7 %copy.25 = f32[1152,2304]{0,1:T(8,128)} copy(f32[1152,2304]{1,0:T(8,128)} %param.9) | data formatting | bytes 21233664 | tf_op args[0]
  13.3 12.7 %copy.26 = f32[1152,2304]{0,1:T(8,128)} copy(f32[1152,2304]{1,0:T(8,128)} %param.10) | data formatting | bytes 21233664 | tf_op args[1]
  26.0 12.7 %copy.28 = f32[1152,2304]{0,1:T(8,128)} copy(f32[1152,2304]{1,0:T(8,128)} %param.11) | data formatting | bytes 21233664 | tf_op args[2]
  38.7 12.7 %copy.29 = f32[1152,2304]{0,1:T(8,128)} copy(f32[1152,2304]{1,0:T(8,128)} %param.12) | data formatting | bytes 21233664 | tf_op args[3]
  51.4 12.7 %copy.31 = f32[1152,2304]{0,1:T(8,128)} copy(f32[1152,2304]{1,0:T(8,128)} %param.13) | data formatting | bytes 21233664 | tf_op args[4]
  64.1 12.7 %copy.32 = f32[1152,2304]{0,1:T(8,128)} copy(f32[1152,2304]{1,0:T(8,128)} %param.14) | data formatting | bytes 21233664 | tf_op args[5]
  76.7 21.5 %abs_reduce_fusion = (f32[2304]{0:T(1024)S(1)}, f32[2304]{0:T(1024)S(1)}, f32[2304]{0:T(1024)S(1)}) fusion(f32[1152,2304]{0,1:T(8,128)} %copy.32, f32[1152]{0:T(1024)S(1)} %broadcast_subtract_fusion, f32[1152,2304]{0,1:T(8,128)} %copy.31, f32[1152]{0:T(1024)S(1)} %copy-done, f32[1152,2304]{0,1:T(8,128)} %copy.29, f32[1152,2304]{0,1:T(8,128)} %copy.28, ...), kind=kLoop, calls=%fused_computation.1 | loop fusion | flops 39806208 | bytes 63737856 | tf_op jit(solution)/shard_map/reduce_max | solution.py:25
  98.3 25.8 %all-reduce.1 = (f32[2304]{0:T(1024)S(1)}, f32[2304]{0:T(1024)S(1)}, f32[2304]{0:T(1024)S(1)}) all-reduce(f32[2304]{0:T(1024)S(1)} %get-tuple-element.9, f32[2304]{0:T(1024)S(1)} %get-tuple-element.8, f32[2304]{0:T(1024)S(1)} %get-tuple-element.7), channel_id=1, replica_groups=mesh['rows'=8,'tp'=4] {'rows'}, use_global_device_ids=true, to_apply=%region_1.0 | all-reduce | flops 6912 | bytes 55296 | tf_op jit(solution)/shard_map/pmax | solution.py:21
  124.1 27.4 %divide_convert_fusion = (bf16[1152,2304]{0,1:T(8,128)(2,1)}, bf16[1152,2304]{0,1:T(8,128)(2,1)}, bf16[1152,2304]{0,1:T(8,128)(2,1)}) fusion(f32[2304]{0:T(1024)S(1)} %get-tuple-element.12, f32[1152,2304]{0,1:T(8,128)} %copy.32, f32[1152]{0:T(1024)S(1)} %broadcast_subtract_fusion, f32[1152,2304]{0,1:T(8,128)} %copy.31, f32[1152]{0:T(1024)S(1)} %copy-done, ...), kind=kLoop, calls=%fused_computation | loop fusion | flops 39813120 | bytes 79663104 | tf_op jit(solution)/shard_map/convert_element_type | solution.py:32
  151.5 65.9 %all_to_all.57 = bf16[1152,8,288]{0,2,1:T(8,128)(2,1)} all-to-all(bf16[1152,8,288]{0,2,1:T(8,128)(2,1)} %bitcast.20), channel_id=1, replica_groups=mesh['rows'=8,'tp'=4] {'rows'}, dimensions={1} | all-to-all | bytes 10616832 | tf_op jit(solution)/shard_map/all_to_all | solution.py:37
  217.5 0.0 copy-start.2
  217.5 64.5 %all_to_all.58 = bf16[1152,8,288]{0,2,1:T(8,128)(2,1)} all-to-all(bf16[1152,8,288]{0,2,1:T(8,128)(2,1)S(1)} %bitcast.19), channel_id=1, replica_groups=mesh['rows'=8,'tp'=4] {'rows'}, dimensions={1} | all-to-all | bytes 10616832 | tf_op jit(solution)/shard_map/all_to_all | solution.py:35
  281.9 4.7 %all-to-all-start.1 = ((bf16[1152,8,288]{0,2,1:T(8,128)(2,1)}), bf16[1152,8,288]{0,2,1:T(8,128)(2,1)}, u32[]{:S(2)}, u32[]{:S(2)}) async-start(bf16[1152,8,288]{0,2,1:T(8,128)(2,1)} %bitcast.16), calls=%async_computation.1 | async-start | bytes 10616832 | tf_op jit(solution)/shard_map/all_to_all | solution.py:36
  286.6 0.0 slice-start
  286.6 0.7 dynamic_slice.10
  287.3 0.7 dynamic_slice.11
  287.9 0.7 dynamic_slice.9
  288.6 0.0 copy-done.1
  288.6 0.3 dynamic-update-slice
  288.8 92.5 %all-reduce = bf16[9216]{0:T(1024)(128)(2,1)} all-reduce(bf16[9216]{0:T(1024)(128)(2,1)S(1)} %dynamic-update-slice), channel_id=1, replica_groups=mesh['rows'=8,'tp'=4] {'rows','tp'}, use_global_device_ids=true, to_apply=%add | all-reduce | flops 9216 | bytes 36864
  381.3 5.9 %copy.36 = bf16[8,36,8,1152]{3,2,0,1:T(8,128)(2,1)} copy(bf16[8,36,8,1152]{3,2,1,0:T(8,128)(2,1)} %bitcast.12) | data formatting | bytes 10616832 | tf_op jit(solution)/shard_map/all_to_all | solution.py:37
  387.2 3.2 copy.34
  390.4 0.0 all-to-all-done.1
  390.4 5.7 %copy.35 = bf16[8,36,8,1152]{3,2,0,1:T(8,128)(2,1)} copy(bf16[8,36,8,1152]{3,2,1,0:T(8,128)(2,1)} %bitcast.8) | data formatting | bytes 10616832 | tf_op jit(solution)/shard_map/all_to_all | solution.py:36
  (16 shorter events, 0.0 us)
Async XLA Ops:
  64.1 12.7 %copy-start = (f32[1152]{0:T(1024)S(1)}, f32[1152]{0:T(1024)}, u32[]{:S(2)}) copy-start(f32[1152]{0:T(1024)} %param.15) | copy-start | bytes 13828
  151.5 65.9 %slice-start.2 = ((s8[5308416]{0:T(1024)(128)(4,1)}), s8[4194304]{0:T(1024)(128)(4,1)S(1)}, s32[]{:S(2)}) async-start(s8[5308416]{0:T(1024)(128)(4,1)} %bitcast.17), calls=%async_computation.5 | async-start | bytes 8388608
  151.5 65.9 %slice-start.3 = ((s8[5308416]{0:T(1024)(128)(4,1)}), s8[1114112]{0:T(1024)(128)(4,1)S(1)}, s32[]{:S(2)}) async-start(s8[5308416]{0:T(1024)(128)(4,1)} %bitcast.17), calls=%async_computation.6 | async-start | bytes 2228224
  217.5 71.1 %copy-start.1 = (f32[288]{0:T(512)S(1)}, f32[288]{0:T(512)}, u32[]{:S(2)}) copy-start(f32[288]{0:T(512)} %param.16) | copy-start | bytes 3460
  217.5 71.1 %copy-start.2 = (f32[288]{0:T(512)S(1)}, f32[288]{0:T(512)}, u32[]{:S(2)}) copy-start(f32[288]{0:T(512)} %param.17) | copy-start | bytes 3460
  281.9 108.4 %all-to-all-start.1 = ((bf16[1152,8,288]{0,2,1:T(8,128)(2,1)}), bf16[1152,8,288]{0,2,1:T(8,128)(2,1)}, u32[]{:S(2)}, u32[]{:S(2)}) async-start(bf16[1152,8,288]{0,2,1:T(8,128)(2,1)} %bitcast.16), calls=%async_computation.1 | async-start | bytes 10616832 | tf_op jit(solution)/shard_map/all_to_all | solution.py:36
  286.6 100.6 %slice-start = ((s8[5308416]{0:T(1024)(128)(4,1)}), s8[1114112]{0:T(1024)(128)(4,1)S(1)}, s32[]{:S(2)}) async-start(s8[5308416]{0:T(1024)(128)(4,1)} %bitcast.13), calls=%async_computation.3 | async-start | bytes 2228224
  381.3 5.9 %slice-start.1 = ((s8[5308416]{0:T(1024)(128)(4,1)}), s8[4194304]{0:T(1024)(128)(4,1)S(1)}, s32[]{:S(2)}) async-start(s8[5308416]{0:T(1024)(128)(4,1)} %bitcast.13), calls=%async_computation.4 | async-start | bytes 8388608
where the time goes:
time: 398 us; the launch traced here: 396 us
  blocking collectives  249 us (63%)
  local copies, waits for them, and re-layouts  93.1 us (23%)
  other arithmetic  49 us (12%)
  starting transfers between devices  4.65 us (1%)
    unnamed x1, blocking collectives  92.5 us
    unnamed x22, local copies, waits for them, and re-layouts  76.4 us
    all_to_all x1, blocking collectives, per_device(): lax.all_to_all(narrow_value, 'rows', split_axis=1, concat_axis=0, tiled=T...  65.9 us
    all_to_all x1, blocking collectives, per_device(): lax.all_to_all(narrow_query, 'rows', split_axis=1, concat_axis=0, tiled=T...  64.5 us
    convert_element_type x1, other arithmetic, per_device(): (whole_value / scale_value).astype(jnp.bfloat16)  27.4 us
    pmax x1, blocking collectives, per_device(): lax.pmax((jnp.max(jnp.abs(whole_query), axis=0), jnp.max(jnp.abs(whole_ke...  25.8 us
    reduce_max x1, other arithmetic, per_device(): jnp.max(jnp.abs(whole_value), axis=0)  21.5 us
  transfers between devices with their start and end apart: 1, of which 0 were waited for; matrix products, arithmetic and copies ran while one was open for 3% of the time, Pallas kernels for 0%

commit v1 on v0

--- a/solution.py
+++ b/solution.py
@@ -2,6 +2,18 @@
 import jax.numpy as jnp
 from jax import lax
 from jax.sharding import PartitionSpec as P
+
+
+def sent_to_each(x, axis, split, join):
+    ways, here = (lax.axis_size(axis), lax.axis_index(axis))
+    width = x.shape[split] // ways
+    turned = jnp.roll(x, -here * width, axis=split)
+    got = [lax.slice_in_dim(turned, 0, width, axis=split)]
+    for far in range(1, ways):
+        sent = lax.slice_in_dim(turned, far * width, (far + 1) * width, axis=split)
+        got.append(lax.ppermute(sent, axis, [(d, (d + far) % ways) for d in range(ways)]))
+    line = jnp.concatenate(got[::-1], axis=join)
+    return jnp.roll(line, (here + 1) * got[0].shape[join], axis=join)
 
 
 def per_device(
@@ -32,7 +44,7 @@
         (whole_value / scale_value).astype(jnp.bfloat16),
     )
     serving_query, serving_key, serving_value = (
-        lax.all_to_all(narrow_query, "rows", split_axis=1, concat_axis=0, tiled=True),
+        sent_to_each(narrow_query, "rows", 1, 0),
         lax.all_to_all(narrow_key, "rows", split_axis=1, concat_axis=0, tiled=True),
         lax.all_to_all(narrow_value, "rows", split_axis=1, concat_axis=0, tiled=True),
     )

time: 398 us -> 397 us (level)
  blocking collectives: 249 us -> 158 us
  waiting for transfers between devices: 0.01 us -> 40 us
  local copies, waits for them, and re-layouts: 93.1 us -> 123 us
  starting transfers between devices: 4.65 us -> 16.7 us
  other arithmetic: 49 us -> 56.9 us
    all_to_all x2 -> x0, blocking collectives: 130 us -> none  [the longest x1 65.9 us: per_device(): lax.all_to_all(narrow_value, 'rows', split_axis=1, concat_axis=0, tiled=T...]
    unnamed x1, blocking collectives: 92.5 us -> 132 us
    all_to_all x0 -> x1, waiting for transfers between devices: none -> 23.8 us  [per_device(): lax.all_to_all(narrow_value, 'rows', split_axis=1, concat_axis=0, tiled=T...]
    unnamed x22 -> x31, local copies, waits for them, and re-layouts: 76.4 us -> 98.2 us
    ppermute x0 -> x7, waiting for transfers between devices: none -> 16.2 us  [sent_to_each(): lax.ppermute(sent, axis, [(d, (d + far) % ways) for d in range(ways)])]
    concatenate x0 -> x1, other arithmetic: none -> 7.97 us  [sent_to_each(): turned = jnp.roll(x, -here * width, axis=split)]
    dynamic_slice x0 -> x1, local copies, waits for them, and re-layouts: none -> 7.06 us  [sent_to_each(): return jnp.roll(line, (here + 1) * got[0].shape[join], axis=join)]
    ppermute x0 -> x7, starting transfers between devices: none -> 6.99 us  [sent_to_each(): lax.ppermute(sent, axis, [(d, (d + far) % ways) for d in range(ways)])]
  transfers between devices with their start and end apart: 1 -> 9, of which waited for: 0 -> 3; matrix products, arithmetic and copies ran while one was open for 3% -> 12% of each run, Pallas kernels for 0% -> 0%
where the time goes in v1:
time: 397 us; the launch traced here: 395 us
  blocking collectives  158 us (40%)
  local copies, waits for them, and re-layouts  123 us (31%)
  other arithmetic  56.9 us (14%)
  waiting for transfers between devices  40 us (10%)
  starting transfers between devices  16.7 us (4%)
    unnamed x1, blocking collectives  132 us
    unnamed x31, local copies, waits for them, and re-layouts  98.2 us
    convert_element_type x1, other arithmetic, per_device(): (whole_value / scale_value).astype(jnp.bfloat16)  27.4 us
    pmax x1, blocking collectives, per_device(): lax.pmax((jnp.max(jnp.abs(whole_query), axis=0), jnp.max(jnp.abs(whole_ke...  25.8 us
    all_to_all x1, waiting for transfers between devices, per_device(): lax.all_to_all(narrow_value, 'rows', split_axis=1, concat_axis=0, tiled=T...  23.8 us
    reduce_max x1, other arithmetic, per_device(): jnp.max(jnp.abs(whole_value), axis=0)  21.6 us
    ppermute x7, waiting for transfers between devices, sent_to_each(): lax.ppermute(sent, axis, [(d, (d + far) % ways) for d in range(ways)])  16.2 us
    concatenate x1, other arithmetic, sent_to_each(): turned = jnp.roll(x, -here * width, axis=split)  7.97 us
  transfers between devices with their start and end apart: 9, of which 3 were waited for; matrix products, arithmetic and copies ran while one was open for 12% of the time, Pallas kernels for 0%

profile of v1, /device:TPU:0, one launch (start us, length us, event | category | flops | bytes accessed | tf_op | source)
XLA Modules:
  0.0 394.8 jit_solution(4211357220524366288)
XLA Ops:
  0.6 12.7 %copy.30 = f32[1152,2304]{0,1:T(8,128)} copy(f32[1152,2304]{1,0:T(8,128)} %param.9) | data formatting | bytes 21233664 | tf_op args[0]
  13.3 12.7 %copy.31 = f32[1152,2304]{0,1:T(8,128)} copy(f32[1152,2304]{1,0:T(8,128)} %param.10) | data formatting | bytes 21233664 | tf_op args[1]
  26.0 12.7 %copy.32 = f32[1152,2304]{0,1:T(8,128)} copy(f32[1152,2304]{1,0:T(8,128)} %param.11) | data formatting | bytes 21233664 | tf_op args[2]
  38.7 12.7 %copy.33 = f32[1152,2304]{0,1:T(8,128)} copy(f32[1152,2304]{1,0:T(8,128)} %param.12) | data formatting | bytes 21233664 | tf_op args[3]
  51.4 12.7 %copy.35 = f32[1152,2304]{0,1:T(8,128)} copy(f32[1152,2304]{1,0:T(8,128)} %param.13) | data formatting | bytes 21233664 | tf_op args[4]
  64.0 12.7 %copy.36 = f32[1152,2304]{0,1:T(8,128)} copy(f32[1152,2304]{1,0:T(8,128)} %param.14) | data formatting | bytes 21233664 | tf_op args[5]
  76.7 21.6 %abs_reduce_fusion = (f32[2304]{0:T(1024)S(1)}, f32[2304]{0:T(1024)S(1)}, f32[2304]{0:T(1024)S(1)}) fusion(f32[1152,2304]{0,1:T(8,128)} %copy.36, f32[1152]{0:T(1024)S(1)} %broadcast_subtract_fusion, f32[1152,2304]{0,1:T(8,128)} %copy.35, f32[1152]{0:T(1024)S(1)} %copy-done.1, f32[1152,2304]{0,1:T(8,128)} %copy.33, f32[1152,2304]{0,1:T(8,128)} %copy.32, ...), kind=kLoop, calls=%fused_computation.3 | loop fusion | flops 39806208 | bytes 63737856 | tf_op jit(solution)/shard_map/reduce_max | solution.py:37
  98.3 25.8 %all-reduce.1 = (f32[2304]{0:T(1024)S(1)}, f32[2304]{0:T(1024)S(1)}, f32[2304]{0:T(1024)S(1)}) all-reduce(f32[2304]{0:T(1024)S(1)} %get-tuple-element.9, f32[2304]{0:T(1024)S(1)} %get-tuple-element.8, f32[2304]{0:T(1024)S(1)} %get-tuple-element.7), channel_id=1, replica_groups=mesh['rows'=8,'tp'=4] {'rows'}, use_global_device_ids=true, to_apply=%region_1.0 | all-reduce | flops 6912 | bytes 55296 | tf_op jit(solution)/shard_map/pmax | solution.py:33
  124.1 27.4 %divide_convert_fusion = (bf16[1152,2304]{0,1:T(8,128)(2,1)}, bf16[1152,2304]{0,1:T(8,128)(2,1)}, bf16[1152,2304]{0,1:T(8,128)(2,1)}) fusion(f32[2304]{0:T(1024)S(1)} %get-tuple-element.12, f32[1152,2304]{0,1:T(8,128)} %copy.36, f32[1152]{0:T(1024)S(1)} %broadcast_subtract_fusion, f32[1152,2304]{0,1:T(8,128)} %copy.35, f32[1152]{0:T(1024)S(1)} %copy-done.1, ...), kind=kLoop, calls=%fused_computation.2 | loop fusion | flops 39813120 | bytes 79663104 | tf_op jit(solution)/shard_map/convert_element_type | solution.py:44
  151.5 4.8 %all-to-all-start = ((bf16[1152,8,288]{0,2,1:T(8,128)(2,1)}), bf16[1152,8,288]{0,2,1:T(8,128)(2,1)}, u32[]{:S(2)}, u32[]{:S(2)}) async-start(bf16[1152,8,288]{0,2,1:T(8,128)(2,1)} %bitcast.9), calls=%async_computation | async-start | bytes 10616832 | tf_op jit(solution)/shard_map/all_to_all | solution.py:48
  156.4 8.0 %fusion = bf16[1152,2304]{0,1:T(8,128)(2,1)S(1)} fusion(s32[]{:T(128)S(6)} %select_n.29, bf16[1152,2304]{0,1:T(8,128)(2,1)} %get-tuple-element.21), kind=kLoop, calls=%fused_computation.11 | loop fusion | flops 10616832 | bytes 10616836 | tf_op jit(solution)/shard_map/jit(_roll_dynamic)/concatenate | solution.py:10
  164.4 2.4 copy-done
  166.7 2.2 fusion.1
  168.9 2.4 collective-permute-start
  175.9 131.7 %all-reduce = bf16[9216]{0:T(1024)(128)(2,1)} all-reduce(bf16[9216]{0:T(1024)(128)(2,1)S(1)} %dynamic-update-slice), channel_id=1, replica_groups=mesh['rows'=8,'tp'=4] {'rows','tp'}, use_global_device_ids=true, to_apply=%add | all-reduce | flops 9216 | bytes 36864
  307.6 2.3 collective-permute-start.5
  313.7 4.9 %all-to-all-start.1 = ((bf16[1152,8,288]{0,2,1:T(8,128)(2,1)}), bf16[1152,8,288]{0,2,1:T(8,128)(2,1)}, u32[]{:S(2)}, u32[]{:S(2)}) async-start(bf16[1152,8,288]{0,2,1:T(8,128)(2,1)} %bitcast.8), calls=%async_computation.1 | async-start | bytes 10616832 | tf_op jit(solution)/shard_map/all_to_all | solution.py:49
  319.5 7.2 %collective-permute-done.5 = bf16[1152,288]{0,1:T(8,128)(2,1)} collective-permute-done((bf16[1152,288]{0,1:T(8,128)(2,1)}, bf16[1152,288]{0,1:T(8,128)(2,1)}, u32[]{:S(2)}, u32[]{:S(2)}) %collective-permute-start.5) | collective-permute-done | bytes 663584 | tf_op jit(solution)/shard_map/ppermute | solution.py:14
  328.7 9.0 %collective-permute-done.6 = bf16[1152,288]{0,1:T(8,128)(2,1)} collective-permute-done((bf16[1152,288]{0,1:T(8,128)(2,1)}, bf16[1152,288]{0,1:T(8,128)(2,1)}, u32[]{:S(2)}, u32[]{:S(2)}) %collective-permute-start.6) | collective-permute-done | bytes 663584 | tf_op jit(solution)/shard_map/ppermute | solution.py:14
  339.8 2.0 slice_dynamic-update-slice_fusion
  352.5 7.1 %constant_dynamic-slice_fusion = bf16[9216,288]{0,1:T(8,128)(2,1)} fusion(bf16[18432,288]{0,1:T(8,128)(2,1)} %slice_dynamic-update-slice_fusion.1, s32[]{:T(128)S(6)} %select_n.31), kind=kLoop, calls=%fused_computation.30 | loop fusion | bytes 10616836 | tf_op jit(solution)/shard_map/jit(_roll_dynamic)/dynamic_slice | solution.py:16
  359.6 5.7 %copy.38 = bf16[8,36,8,1152]{3,2,0,1:T(8,128)(2,1)} copy(bf16[8,36,8,1152]{3,2,1,0:T(8,128)(2,1)} %bitcast.4) | data formatting | bytes 10616832 | tf_op jit(solution)/shard_map/all_to_all | solution.py:48
  365.3 23.8 %all-to-all-done.1 = bf16[1152,8,288]{0,2,1:T(8,128)(2,1)} async-done(((bf16[1152,8,288]{0,2,1:T(8,128)(2,1)}), bf16[1152,8,288]{0,2,1:T(8,128)(2,1)}, u32[]{:S(2)}, u32[]{:S(2)}) %all-to-all-start.1) | async-done | bytes 5308448 | tf_op jit(solution)/shard_map/all_to_all | solution.py:49
  389.1 5.7 %copy.39 = bf16[8,36,8,1152]{3,2,0,1:T(8,128)(2,1)} copy(bf16[8,36,8,1152]{3,2,1,0:T(8,128)(2,1)} %bitcast.6) | data formatting | bytes 10616832 | tf_op jit(solution)/shard_map/all_to_all | solution.py:49
  (40 shorter events, 24.1 us)
Async XLA Ops:
  64.0 12.7 %copy-start.1 = (f32[1152]{0:T(1024)S(1)}, f32[1152]{0:T(1024)}, u32[]{:S(2)}) copy-start(f32[1152]{0:T(1024)} %param.15) | copy-start | bytes 13828
  151.5 162.2 %all-to-all-start = ((bf16[1152,8,288]{0,2,1:T(8,128)(2,1)}), bf16[1152,8,288]{0,2,1:T(8,128)(2,1)}, u32[]{:S(2)}, u32[]{:S(2)}) async-start(bf16[1152,8,288]{0,2,1:T(8,128)(2,1)} %bitcast.9), calls=%async_computation | async-start | bytes 10616832 | tf_op jit(solution)/shard_map/all_to_all | solution.py:48
  156.3 19.3 %copy-start.2 = (f32[288]{0:T(512)S(1)}, f32[288]{0:T(512)}, u32[]{:S(2)}) copy-start(f32[288]{0:T(512)} %param.16) | copy-start | bytes 3460
  156.3 19.3 %copy-start.3 = (f32[288]{0:T(512)S(1)}, f32[288]{0:T(512)}, u32[]{:S(2)}) copy-start(f32[288]{0:T(512)} %param.17) | copy-start | bytes 3460
  164.3 2.4 copy-start
  168.9 138.7 %collective-permute-start = (bf16[1152,288]{0,1:T(8,128)(2,1)}, bf16[1152,288]{0,1:T(8,128)(2,1)S(1)}, u32[]{:S(2)}, u32[]{:S(2)}) collective-permute-start(bf16[1152,288]{0,1:T(8,128)(2,1)} %get-tuple-element.19), channel_id=1, source_target_pairs={{0,28},{4,0},{8,4},{12,8},{16,12},{20,16},{24,20},{28,24},{1,29},{... | collective-permute-start | bytes 1990664 | tf_op jit(solution)/shard_map/ppermute | solution.py:14
  171.3 139.5 %collective-permute-start.1 = (bf16[1152,288]{0,1:T(8,128)(2,1)}, bf16[1152,288]{0,1:T(8,128)(2,1)S(1)}, u32[]{:S(2)}, u32[]{:S(2)}) collective-permute-start(bf16[1152,288]{0,1:T(8,128)(2,1)} %get-tuple-element.18), channel_id=1, source_target_pairs={{0,24},{4,28},{8,0},{12,4},{16,8},{20,12},{24,16},{28,20},{1,25},{... | collective-permute-start | bytes 1990664 | tf_op jit(solution)/shard_map/ppermute | solution.py:14
  171.9 139.9 %collective-permute-start.2 = (bf16[1152,288]{0,1:T(8,128)(2,1)}, bf16[1152,288]{0,1:T(8,128)(2,1)S(1)}, u32[]{:S(2)}, u32[]{:S(2)}) collective-permute-start(bf16[1152,288]{0,1:T(8,128)(2,1)} %get-tuple-element.17), channel_id=1, source_target_pairs={{0,20},{4,24},{8,28},{12,0},{16,4},{20,8},{24,12},{28,16},{1,21},{... | collective-permute-start | bytes 1990664 | tf_op jit(solution)/shard_map/ppermute | solution.py:14
  172.0 140.8 %collective-permute-start.3 = (bf16[1152,288]{0,1:T(8,128)(2,1)}, bf16[1152,288]{0,1:T(8,128)(2,1)S(1)}, u32[]{:S(2)}, u32[]{:S(2)}) collective-permute-start(bf16[1152,288]{0,1:T(8,128)(2,1)} %get-tuple-element.16), channel_id=1, source_target_pairs={{0,16},{4,20},{8,24},{12,28},{16,0},{20,4},{24,8},{28,12},{1,17},{... | collective-permute-start | bytes 1990664 | tf_op jit(solution)/shard_map/ppermute | solution.py:14
  173.4 145.1 %collective-permute-start.4 = (bf16[1152,288]{0,1:T(8,128)(2,1)}, bf16[1152,288]{0,1:T(8,128)(2,1)S(1)}, u32[]{:S(2)}, u32[]{:S(2)}) collective-permute-start(bf16[1152,288]{0,1:T(8,128)(2,1)} %get-tuple-element.15), channel_id=1, source_target_pairs={{0,12},{4,16},{8,20},{12,24},{16,28},{20,0},{24,4},{28,8},{1,13},{... | collective-permute-start | bytes 1990664 | tf_op jit(solution)/shard_map/ppermute | solution.py:14
  307.6 19.1 %collective-permute-start.5 = (bf16[1152,288]{0,1:T(8,128)(2,1)}, bf16[1152,288]{0,1:T(8,128)(2,1)}, u32[]{:S(2)}, u32[]{:S(2)}) collective-permute-start(bf16[1152,288]{0,1:T(8,128)(2,1)} %get-tuple-element.14), channel_id=1, source_target_pairs={{0,8},{4,12},{8,16},{12,20},{16,24},{20,28},{24,0},{28,4},{1,9},{5... | collective-permute-start | bytes 1990664 | tf_op jit(solution)/shard_map/ppermute | solution.py:14
  310.8 26.9 %collective-permute-start.6 = (bf16[1152,288]{0,1:T(8,128)(2,1)}, bf16[1152,288]{0,1:T(8,128)(2,1)}, u32[]{:S(2)}, u32[]{:S(2)}) collective-permute-start(bf16[1152,288]{0,1:T(8,128)(2,1)} %get-tuple-element.13), channel_id=1, source_target_pairs={{0,4},{4,8},{8,12},{12,16},{16,20},{20,24},{24,28},{28,0},{1,5},{5... | collective-permute-start | bytes 1990664 | tf_op jit(solution)/shard_map/ppermute | solution.py:14
  313.7 75.5 %all-to-all-start.1 = ((bf16[1152,8,288]{0,2,1:T(8,128)(2,1)}), bf16[1152,8,288]{0,2,1:T(8,128)(2,1)}, u32[]{:S(2)}, u32[]{:S(2)}) async-start(bf16[1152,8,288]{0,2,1:T(8,128)(2,1)} %bitcast.8), calls=%async_computation.1 | async-start | bytes 10616832 | tf_op jit(solution)/shard_map/all_to_all | solution.py:49
